TPU v7x, 32 devices: a whole 2x2x4 slice. The times are simulated.
32 devices in a mesh: lat: 4 (over x, core), src: 8 (over z, y).
Axes of the slice: x: 2, y: 2, z: 4, core: 2. Of those that a mesh axis runs over, the one named last changes fastest.
Arguments:
- fine_residual: bfloat16 [8, 16, 256, 2048], P('lat', 'src'), may hold values from -6 to 6
- basis: bfloat16 [8, 16, 2048, 128], P('lat', 'src'), may hold values from -0.25 to 0.25
- diag_inverse: bfloat16 [8, 16, 128, 128], P('lat', 'src'), may hold values from -0.32 to 1.7, as said below
- hoppings: bfloat16 [8, 16, 8, 128, 128], P('lat', 'src'), may hold values from -0.125 to 0.125
- neighbours: int32 [16, 6], replicated, may hold values from 0 to 15, as said below
- aggregation: int32 [8, 16], P('lat', 'src'), may hold values from 0 to 15, as said below
Outputs:
- correction: bfloat16 [8, 16, 256, 2048], P('lat', 'src')
Inputs may be any that keep to these rules, and one draw needn't show every extreme that they name: `diag_inverse`: a site's diagonal inverse is one on the diagonal within a fifth (two fifths in some draws) plus independent off-diagonal entries. The spatial sites form a periodic grid of 8 by 1 by 2 sites, site (x, y, z) having index (x * 1 + y) * 2 + z; columns 2k and 2k+1 hold the two periodic neighbours along grid direction k, one step up and one step down, in an order drawn for each k. `aggregation`: in each row, every aligned block of 2 entries is a permutation of that block's own column indices.
All inputs are finite; a program needn't handle non-finite values.
Results may differ from a plain program's by a relative error of at most 0.0075.
Values may be sent and summed in bfloat16 or wider, within the bound.
A program may use at most 128 MiB of HBM per device.

v0:
```python
import jax
import jax.numpy as jnp
from jax import lax
from jax.sharding import PartitionSpec as P

SWEEPS = 3


damping = 0.8


def with_halo(cells, sides, width):
    for axis, dim in sides:
        count = lax.axis_size(axis)
        head = lax.slice_in_dim(cells, 0, width, axis=dim)
        tail = lax.slice_in_dim(cells, cells.shape[dim] - width, cells.shape[dim], axis=dim)
        cells = jnp.concatenate(
            [
                lax.ppermute(tail, axis, [(i, (i + 1) % count) for i in range(count)]),
                cells,
                lax.ppermute(head, axis, [((i + 1) % count, i) for i in range(count)]),
            ],
            axis=dim,
        )
    return cells


def hop_terms(source, neighbour_rows, padded, hops):
    spatial = jnp.take(source, neighbour_rows, axis=1)
    upper_time = padded[2:][:, :, None]
    lower_time = padded[:-2][:, :, None]
    stacked = jnp.concatenate([spatial, upper_time, lower_time], axis=2)
    return jnp.einsum("tsknc,tskcd->tsnd", stacked, hops, preferred_element_type=jnp.float32)


def first_sweep(coarse_rhs, inverse_blocks):
    applied = jnp.einsum(
        "tsnc,tscd->tsnd", coarse_rhs, inverse_blocks, preferred_element_type=jnp.float32
    )
    return (damping * applied).astype(jnp.bfloat16)


def later_sweep(coarse_rhs, iterate, hop_sum, inverse_blocks):
    difference = (coarse_rhs.astype(jnp.float32) - hop_sum).astype(jnp.bfloat16)
    applied = jnp.einsum(
        "tsnc,tscd->tsnd", difference, inverse_blocks, preferred_element_type=jnp.float32
    )
    return ((1.0 - damping) * iterate.astype(jnp.float32) + damping * applied).astype(jnp.bfloat16)


def body(fine_residual, basis, diag_inverse, hoppings, neighbours, aggregation):
    slab_width = basis.shape[1]
    all_sites = neighbours.shape[0]
    restricted = jnp.einsum(
        "tsnr,tsrc->tsnc", fine_residual, basis, preferred_element_type=jnp.float32
    ).astype(jnp.bfloat16)
    within = aggregation - lax.axis_index("src") * slab_width
    inverse = jnp.argsort(within, axis=1)
    coarse_rhs = jnp.take_along_axis(restricted, inverse[:, :, None, None], axis=1)
    first_row = lax.axis_index("src") * slab_width
    neighbour_rows = lax.dynamic_slice_in_dim(neighbours, first_row, slab_width, 0)
    local_rows = (neighbour_rows - first_row + slab_width + all_sites) % all_sites
    iterate = first_sweep(coarse_rhs, diag_inverse)
    for sweep_index in range(SWEEPS - 1):
        padded = with_halo(iterate, (("lat", 0),), 1)
        extended = with_halo(iterate, (("src", 1),), slab_width)
        hop_sum = hop_terms(extended, local_rows, padded, hoppings)
        iterate = later_sweep(coarse_rhs, iterate, hop_sum, diag_inverse)
    gathered = jnp.take_along_axis(iterate, within[:, :, None, None], axis=1)
    return jnp.einsum(
        "tsnc,tsrc->tsnr", gathered, basis, preferred_element_type=jnp.float32
    ).astype(jnp.bfloat16)


def solution(mesh):
    return jax.shard_map(
        body,
        mesh=mesh,
        in_specs=(
            P("lat", "src", None, None),
            P("lat", "src", None, None),
            P("lat", "src", None, None),
            P("lat", "src", None, None, None),
            P(),
            P("lat", "src"),
        ),
        out_specs=P("lat", "src", None, None),
        check_vma=False,
    )
```

profile of v0, /device:TPU:0, one launch (start us, length us, event | category | flops | bytes accessed | tf_op | source)
XLA Modules:
  0.0 56.0 jit_solution(13263402525408739929)
XLA Ops:
  0.0 0.9 %copy.15 = s32[2,2]{0,1:T(2,128)S(1)} copy(s32[2,2]{1,0:T(2,128)} %param.15) | data formatting | bytes 32 | tf_op args[5]
  0.9 0.6 %sort.17 = (s32[2,2]{0,1:T(2,128)}, s32[2,2]{0,1:T(2,128)S(1)}) sort(s32[2,2]{0,1:T(2,128)S(1)} %broadcast_subtract_fusion, s32[2,2]{0,1:T(2,128)S(1)} %iota.7), dimensions={1}, to_apply=%region_0.0 | sort | flops 8 | bytes 64 | tf_op jit(solution)/shard_map/jit(argsort)/sort | solution.py:58
  1.5 0.1 copy.17
  1.7 3.5 %convolution_convert_fusion.1 = bf16[2,2,256,128]{3,2,1,0:T(8,128)(2,1)S(1)} fusion(bf16[2,2,256,2048]{3,2,1,0:T(8,128)(2,1)} %param.10, bf16[2,2,2048,128]{3,2,1,0:T(8,128)(2,1)S(1)} %copy-done), kind=kOutput, calls=%fused_computation.26 | convolution fusion | flops 537001984 | bytes 6553600 | tf_op jit(solution)/shard_map/tsnr,tsrc->tsnc/dot_general | solution.py:54
  5.2 0.6 %gather_fusion = bf16[4,256,128]{2,1,0:T(8,128)(2,1)S(1)} fusion(bf16[2,2,256,128]{3,2,1,0:T(8,128)(2,1)S(1)} %convolution_convert_fusion.1, s32[4]{0:T(128)S(1)} %reshape.67), kind=kCustom, calls=%fused_computation.clone | custom fusion | bytes 524320 | tf_op jit(solution)/shard_map/jit(take_along_axis)/gather | solution.py:59
  5.8 0.3 fusion.26
  6.1 6.1 %collective-permute-start.1 = (bf16[2,2,256,128]{3,2,1,0:T(8,128)(2,1)S(1)}, bf16[2,2,256,128]{3,2,1,0:T(8,128)(2,1)S(1)}, u32[]{:S(2)}, u32[]{:S(2)}) collective-permute-start(bf16[2,2,256,128]{3,2,1,0:T(8,128)(2,1)S(1)} %fusion.26), channel_id=1, source_target_pairs={{1,0},{2,1},{3,2},{4,3},{5,4},{6,5},{7,6},{0,7},{9,8},{10,9},{11,1... | collective-permute-start | bytes 786440 | tf_op jit(solution)/shard_map/ppermute | solution.py:21
  12.2 0.7 %collective-permute-start.2 = (bf16[1,2,256,128]{3,2,1,0:T(8,128)(2,1)S(1)}, bf16[1,2,256,128]{3,2,1,0:T(8,128)(2,1)S(1)}, u32[]{:S(2)}, u32[]{:S(2)}) collective-permute-start(bf16[1,2,256,128]{3,2,1,0:T(8,128)(2,1)S(1)} %get-tuple-element.17), channel_id=1, source_target_pairs={{8,0},{16,8},{24,16},{0,24},{9,1},{17,9},{25,17},{1,25},{10,2},{18... | collective-permute-start | bytes 393224 | tf_op jit(solution)/shard_map/ppermute | solution.py:21
  12.9 0.1 copy.16
  13.2 0.1 copy.18
  13.3 0.1 copy.19
  13.5 3.0 %collective-permute-done.2 = bf16[1,2,256,128]{3,2,1,0:T(8,128)(2,1)S(1)} collective-permute-done((bf16[1,2,256,128]{3,2,1,0:T(8,128)(2,1)S(1)}, bf16[1,2,256,128]{3,2,1,0:T(8,128)(2,1)S(1)}, u32[]{:S(2)}, u32[]{:S(2)}) %collective-permute-start.2) | collective-permute-done | bytes 131104 | tf_op jit(solution)/shard_map/ppermute | solution.py:21
  16.5 1.6 %collective-permute-done.3 = bf16[1,2,256,128]{3,2,1,0:T(8,128)(2,1)S(1)} collective-permute-done((bf16[1,2,256,128]{3,2,1,0:T(8,128)(2,1)S(1)}, bf16[1,2,256,128]{3,2,1,0:T(8,128)(2,1)S(1)}, u32[]{:S(2)}, u32[]{:S(2)}) %collective-permute-start.3) | collective-permute-done | bytes 131104 | tf_op jit(solution)/shard_map/ppermute | solution.py:19
  18.1 0.8 %fusion.36 = (bf16[2,2,1,256,128]{4,3,1,0,2:T(8,128)(2,1)}, bf16[2,2,1,256,128]{4,3,1,0,2:T(8,128)(2,1)}) fusion(bf16[1,2,256,128]{3,2,1,0:T(8,128)(2,1)S(1)} %collective-permute-done.2, bf16[2,2,256,128]{3,2,1,0:T(8,128)(2,1)S(1)} %fusion.26, bf16[1,2,256,128]{3,2,1,0:T(8,128)(2,1)S(1)} %collective-permute-done.3), kind=kLoop, calls=%fused_computation.39 | loop fusion | flops 262144 | bytes 1048576 | tf_op jit(solution)/shard_map/broadcast_in_dim | solution.py:30
  19.0 0.7 %copy-done.3 = bf16[2,2,256,128]{3,2,1,0:T(8,128)(2,1)} copy-done((bf16[2,2,256,128]{3,2,1,0:T(8,128)(2,1)}, bf16[2,2,256,128]{3,2,1,0:T(8,128)(2,1)S(1)}, u32[]{:S(2)}) %copy-start.3) | copy-done | bytes 262168
  19.7 3.1 %collective-permute-done = bf16[2,2,256,128]{3,2,1,0:T(8,128)(2,1)} collective-permute-done((bf16[2,2,256,128]{3,2,1,0:T(8,128)(2,1)S(1)}, bf16[2,2,256,128]{3,2,1,0:T(8,128)(2,1)}, u32[]{:S(2)}, u32[]{:S(2)}) %collective-permute-start) | collective-permute-done | bytes 262176 | tf_op jit(solution)/shard_map/ppermute | solution.py:19
  22.8 1.1 %pad_maximum_fusion.2 = bf16[2,6,256,128]{3,2,1,0:T(8,128)(2,1)S(1)} fusion(bf16[2,2,256,128]{3,2,1,0:T(8,128)(2,1)} %copy-done.3, bf16[2,2,256,128]{3,2,1,0:T(8,128)(2,1)S(1)} %fusion.26, bf16[2,2,256,128]{3,2,1,0:T(8,128)(2,1)} %collective-permute-done), kind=kLoop, calls=%fused_computation.28 | loop fusion | flops 786432 | bytes 1572864 | tf_op jit(solution)/shard_map/concatenate | solution.py:17
  23.9 1.9 %gather_fusion.1 = bf16[12,2,256,128]{3,2,1,0:T(8,128)(2,1)} fusion(bf16[2,6,256,128]{3,2,1,0:T(8,128)(2,1)S(1)} %pad_maximum_fusion.2, s32[1024]{0:T(1024)S(1)} %pad_clamp_fusion), kind=kCustom, calls=%fused_computation.1.clone | custom fusion | bytes 3145776 | tf_op jit(solution)/shard_map/jit(_take)/gather | solution.py:29
  25.8 2.8 %select_bitcast_fusion.1 = bf16[2,2,6,256,128]{4,3,0,2,1:T(8,128)(2,1)} fusion(bf16[2,6,2,256,128]{4,3,2,1,0:T(8,128)(2,1)} %bitcast.67, pred[2,6]{1,0:T(4,128)(4,1)S(1)} %copy.18), kind=kLoop, calls=%fused_computation.12 | loop fusion | flops 786432 | bytes 3145740 | tf_op jit(solution)/shard_map/jit(_take)/select_n | solution.py:29
  28.7 2.5 %fusion.24 = bf16[2,2,256,128]{3,2,1,0:T(8,128)(2,1)S(1)} fusion(bf16[2,2,128,128]{3,2,1,0:T(8,128)(2,1)S(1)} %copy-done.10, bf16[2,2,8,128,128]{4,3,2,1,0:T(8,128)(2,1)} %param.13, bf16[2,2,256,128]{3,2,1,0:T(8,128)(2,1)S(1)} %fusion.26, bf16[2,2,256,128]{3,2,1,0:T(8,128)(2,1)S(1)} %bitcast.70, pred[2,2]{1,0:T(4,128)(4,1)} %copy-done.11, ...), kind=kOutput, calls=%fused_computation.24 | convolution fusion | flops 309460992 | bytes 4063236 | tf_op jit(solution)/shard_map/tsnc,tscd->tsnd/dot_general | solution.py:45
  31.2 3.5 %collective-permute-start.5 = (bf16[2,2,256,128]{3,2,1,0:T(8,128)(2,1)S(1)}, bf16[2,2,256,128]{3,2,1,0:T(8,128)(2,1)S(1)}, u32[]{:S(2)}, u32[]{:S(2)}) collective-permute-start(bf16[2,2,256,128]{3,2,1,0:T(8,128)(2,1)S(1)} %fusion.24), channel_id=1, source_target_pairs={{1,0},{2,1},{3,2},{4,3},{5,4},{6,5},{7,6},{0,7},{9,8},{10,9},{11,1... | collective-permute-start | bytes 786440 | tf_op jit(solution)/shard_map/ppermute | solution.py:21
  34.7 0.5 collective-permute-start.7
  35.2 2.5 %collective-permute-done.6 = bf16[1,2,256,128]{3,2,1,0:T(8,128)(2,1)S(1)} collective-permute-done((bf16[1,2,256,128]{3,2,1,0:T(8,128)(2,1)S(1)}, bf16[1,2,256,128]{3,2,1,0:T(8,128)(2,1)S(1)}, u32[]{:S(2)}, u32[]{:S(2)}) %collective-permute-start.6) | collective-permute-done | bytes 131104 | tf_op jit(solution)/shard_map/ppermute | solution.py:21
  37.7 2.8 %collective-permute-done.7 = bf16[1,2,256,128]{3,2,1,0:T(8,128)(2,1)S(1)} collective-permute-done((bf16[1,2,256,128]{3,2,1,0:T(8,128)(2,1)S(1)}, bf16[1,2,256,128]{3,2,1,0:T(8,128)(2,1)S(1)}, u32[]{:S(2)}, u32[]{:S(2)}) %collective-permute-start.7) | collective-permute-done | bytes 131104 | tf_op jit(solution)/shard_map/ppermute | solution.py:19
  40.5 0.8 %fusion.34 = (bf16[2,2,1,256,128]{4,3,1,0,2:T(8,128)(2,1)}, bf16[2,2,1,256,128]{4,3,1,0,2:T(8,128)(2,1)}) fusion(bf16[1,2,256,128]{3,2,1,0:T(8,128)(2,1)S(1)} %collective-permute-done.6, bf16[2,2,256,128]{3,2,1,0:T(8,128)(2,1)S(1)} %fusion.24, bf16[1,2,256,128]{3,2,1,0:T(8,128)(2,1)S(1)} %collective-permute-done.7), kind=kLoop, calls=%fused_computation.35 | loop fusion | flops 262144 | bytes 1048576 | tf_op jit(solution)/shard_map/broadcast_in_dim | solution.py:30
  41.3 3.1 %collective-permute-done.5 = bf16[2,2,256,128]{3,2,1,0:T(8,128)(2,1)S(1)} collective-permute-done((bf16[2,2,256,128]{3,2,1,0:T(8,128)(2,1)S(1)}, bf16[2,2,256,128]{3,2,1,0:T(8,128)(2,1)S(1)}, u32[]{:S(2)}, u32[]{:S(2)}) %collective-permute-start.5) | collective-permute-done | bytes 262176 | tf_op jit(solution)/shard_map/ppermute | solution.py:21
  44.4 0.2 collective-permute-done.4
  44.7 1.9 %gather_fusion.2 = bf16[12,2,256,128]{3,2,1,0:T(8,128)(2,1)} fusion(bf16[2,6,256,128]{3,2,1,0:T(8,128)(2,1)S(1)} %pad_maximum_fusion.3, s32[1024]{0:T(1024)S(1)} %pad_clamp_fusion), kind=kCustom, calls=%fused_computation.3.clone | custom fusion | bytes 3145776 | tf_op jit(solution)/shard_map/jit(_take)/gather | solution.py:29
  46.6 2.8 %select_bitcast_fusion = bf16[2,2,6,256,128]{4,3,0,2,1:T(8,128)(2,1)} fusion(bf16[2,6,2,256,128]{4,3,2,1,0:T(8,128)(2,1)} %bitcast.66, pred[2,6]{1,0:T(4,128)(4,1)S(1)} %copy.18), kind=kLoop, calls=%fused_computation.11 | loop fusion | flops 786432 | bytes 3145740 | tf_op jit(solution)/shard_map/jit(_take)/select_n | solution.py:29
  49.5 2.5 %fusion.25 = bf16[2,2,256,128]{3,2,1,0:T(8,128)(2,1)S(1)} fusion(bf16[2,2,128,128]{3,2,1,0:T(8,128)(2,1)} %param.12, bf16[2,2,8,128,128]{4,3,2,1,0:T(8,128)(2,1)} %param.13, bf16[2,2,256,128]{3,2,1,0:T(8,128)(2,1)S(1)} %fusion.24, bf16[2,2,256,128]{3,2,1,0:T(8,128)(2,1)S(1)} %bitcast.71, pred[2,2]{1,0:T(4,128)(4,1)S(1)} %copy-done.12, ...), kind=kOutput, calls=%fused_computation.25 | convolution fusion | flops 309460992 | bytes 4063236 | tf_op jit(solution)/shard_map/tsnc,tscd->tsnd/dot_general | solution.py:45
  52.0 0.6 %gather_fusion.3 = bf16[4,256,128]{2,1,0:T(8,128)(2,1)S(1)} fusion(bf16[2,2,256,128]{3,2,1,0:T(8,128)(2,1)S(1)} %fusion.25, s32[4]{0:T(128)S(1)} %reshape.80), kind=kCustom, calls=%fused_computation.2.clone | custom fusion | bytes 524320 | tf_op jit(solution)/shard_map/jit(take_along_axis)/gather | solution.py:69
  52.6 3.3 %convolution_convert_fusion = bf16[2,2,256,2048]{3,2,1,0:T(8,128)(2,1)} fusion(bf16[2,2,2048,128]{3,2,1,0:T(8,128)(2,1)S(1)} %copy-done, bf16[2,2,256,128]{3,2,1,0:T(8,128)(2,1)S(1)} %bitcast.68, pred[2,2]{1,0:T(4,128)(4,1)S(1)} %and_bitcast_fusion), kind=kOutput, calls=%fused_computation.4 | convolution fusion | flops 539099136 | bytes 6553604 | tf_op jit(solution)/shard_map/tsnc,tsrc->tsnr/dot_general | solution.py:70
  (44 shorter events, 0.6 us)
Async XLA Ops:
  0.0 1.7 %copy-start = (bf16[2,2,2048,128]{3,2,1,0:T(8,128)(2,1)S(1)}, bf16[2,2,2048,128]{3,2,1,0:T(8,128)(2,1)}, u32[]{:S(2)}) copy-start(bf16[2,2,2048,128]{3,2,1,0:T(8,128)(2,1)} %param.11) | copy-start | bytes 6291460
  1.6 4.2 %copy-start.11 = (pred[2,2]{1,0:T(4,128)(4,1)}, pred[2,2]{1,0:T(4,128)(4,1)S(1)}, u32[]{:S(2)}) copy-start(pred[2,2]{1,0:T(4,128)(4,1)S(1)} %and_bitcast_fusion.1) | copy-start | bytes 16
  1.7 4.1 %copy-start.9 = (bf16[2,2,128,128]{3,2,1,0:T(8,128)(2,1)S(1)}, bf16[2,2,128,128]{3,2,1,0:T(8,128)(2,1)}, u32[]{:S(2)}) copy-start(bf16[2,2,128,128]{3,2,1,0:T(8,128)(2,1)} %param.12) | copy-start | bytes 393220
  1.7 11.3 %copy-start.8 = (s32[16,6]{0,1:T(8,128)S(1)}, s32[16,6]{0,1:T(8,128)}, u32[]{:S(2)}) copy-start(s32[16,6]{0,1:T(8,128)} %param.14) | copy-start | bytes 1156
  5.8 22.9 %copy-start.1 = (bf16[4,256,128]{2,1,0:T(8,128)(2,1)}, bf16[4,256,128]{2,1,0:T(8,128)(2,1)S(1)}, u32[]{:S(2)}) copy-start(bf16[4,256,128]{2,1,0:T(8,128)(2,1)S(1)} %gather_fusion) | copy-start | bytes 786436
  6.1 12.9 %collective-permute-start.1 = (bf16[2,2,256,128]{3,2,1,0:T(8,128)(2,1)S(1)}, bf16[2,2,256,128]{3,2,1,0:T(8,128)(2,1)S(1)}, u32[]{:S(2)}, u32[]{:S(2)}) collective-permute-start(bf16[2,2,256,128]{3,2,1,0:T(8,128)(2,1)S(1)} %fusion.26), channel_id=1, source_target_pairs={{1,0},{2,1},{3,2},{4,3},{5,4},{6,5},{7,6},{0,7},{9,8},{10,9},{11,1... | collective-permute-start | bytes 786440 | tf_op jit(solution)/shard_map/ppermute | solution.py:21
  12.2 10.6 %collective-permute-start = (bf16[2,2,256,128]{3,2,1,0:T(8,128)(2,1)S(1)}, bf16[2,2,256,128]{3,2,1,0:T(8,128)(2,1)}, u32[]{:S(2)}, u32[]{:S(2)}) collective-permute-start(bf16[2,2,256,128]{3,2,1,0:T(8,128)(2,1)S(1)} %fusion.26), channel_id=1, source_target_pairs={{0,1},{1,2},{2,3},{3,4},{4,5},{5,6},{6,7},{7,0},{8,9},{9,10},{10,1... | collective-permute-start | bytes 786440 | tf_op jit(solution)/shard_map/ppermute | solution.py:19
  12.2 4.3 %collective-permute-start.2 = (bf16[1,2,256,128]{3,2,1,0:T(8,128)(2,1)S(1)}, bf16[1,2,256,128]{3,2,1,0:T(8,128)(2,1)S(1)}, u32[]{:S(2)}, u32[]{:S(2)}) collective-permute-start(bf16[1,2,256,128]{3,2,1,0:T(8,128)(2,1)S(1)} %get-tuple-element.17), channel_id=1, source_target_pairs={{8,0},{16,8},{24,16},{0,24},{9,1},{17,9},{25,17},{1,25},{10,2},{18... | collective-permute-start | bytes 393224 | tf_op jit(solution)/shard_map/ppermute | solution.py:21
  12.9 5.2 %collective-permute-start.3 = (bf16[1,2,256,128]{3,2,1,0:T(8,128)(2,1)S(1)}, bf16[1,2,256,128]{3,2,1,0:T(8,128)(2,1)S(1)}, u32[]{:S(2)}, u32[]{:S(2)}) collective-permute-start(bf16[1,2,256,128]{3,2,1,0:T(8,128)(2,1)S(1)} %get-tuple-element.18), channel_id=1, source_target_pairs={{0,8},{8,16},{16,24},{24,0},{1,9},{9,17},{17,25},{25,1},{2,10},{10... | collective-permute-start | bytes 393224 | tf_op jit(solution)/shard_map/ppermute | solution.py:19
  19.0 0.7 %copy-start.3 = (bf16[2,2,256,128]{3,2,1,0:T(8,128)(2,1)}, bf16[2,2,256,128]{3,2,1,0:T(8,128)(2,1)S(1)}, u32[]{:S(2)}) copy-start(bf16[2,2,256,128]{3,2,1,0:T(8,128)(2,1)S(1)} %collective-permute-done.1) | copy-start | bytes 786436
  25.8 2.8 %copy-start.6 = (bf16[2,2,1,256,128]{4,3,1,0,2:T(8,128)(2,1)S(1)}, bf16[2,2,1,256,128]{4,3,1,0,2:T(8,128)(2,1)}, u32[]{:S(2)}) copy-start(bf16[2,2,1,256,128]{4,3,1,0,2:T(8,128)(2,1)} %get-tuple-element.15) | copy-start | bytes 786436
  25.8 2.8 %copy-start.7 = (bf16[2,2,1,256,128]{4,3,1,0,2:T(8,128)(2,1)S(1)}, bf16[2,2,1,256,128]{4,3,1,0,2:T(8,128)(2,1)}, u32[]{:S(2)}) copy-start(bf16[2,2,1,256,128]{4,3,1,0,2:T(8,128)(2,1)} %get-tuple-element.16) | copy-start | bytes 786436
  25.8 2.8 %copy-start.10 = (bf16[2,2,128,128]{3,2,1,0:T(8,128)(2,1)S(1)}, bf16[2,2,128,128]{3,2,1,0:T(8,128)(2,1)}, u32[]{:S(2)}) copy-start(bf16[2,2,128,128]{3,2,1,0:T(8,128)(2,1)} %param.12) | copy-start | bytes 393220
  31.2 13.2 %collective-permute-start.5 = (bf16[2,2,256,128]{3,2,1,0:T(8,128)(2,1)S(1)}, bf16[2,2,256,128]{3,2,1,0:T(8,128)(2,1)S(1)}, u32[]{:S(2)}, u32[]{:S(2)}) collective-permute-start(bf16[2,2,256,128]{3,2,1,0:T(8,128)(2,1)S(1)} %fusion.24), channel_id=1, source_target_pairs={{1,0},{2,1},{3,2},{4,3},{5,4},{6,5},{7,6},{0,7},{9,8},{10,9},{11,1... | collective-permute-start | bytes 786440 | tf_op jit(solution)/shard_map/ppermute | solution.py:21
  34.7 9.9 %collective-permute-start.4 = (bf16[2,2,256,128]{3,2,1,0:T(8,128)(2,1)S(1)}, bf16[2,2,256,128]{3,2,1,0:T(8,128)(2,1)S(1)}, u32[]{:S(2)}, u32[]{:S(2)}) collective-permute-start(bf16[2,2,256,128]{3,2,1,0:T(8,128)(2,1)S(1)} %fusion.24), channel_id=1, source_target_pairs={{0,1},{1,2},{2,3},{3,4},{4,5},{5,6},{6,7},{7,0},{8,9},{9,10},{10,1... | collective-permute-start | bytes 786440 | tf_op jit(solution)/shard_map/ppermute | solution.py:19
  34.7 3.0 %collective-permute-start.6 = (bf16[1,2,256,128]{3,2,1,0:T(8,128)(2,1)S(1)}, bf16[1,2,256,128]{3,2,1,0:T(8,128)(2,1)S(1)}, u32[]{:S(2)}, u32[]{:S(2)}) collective-permute-start(bf16[1,2,256,128]{3,2,1,0:T(8,128)(2,1)S(1)} %get-tuple-element.13), channel_id=1, source_target_pairs={{8,0},{16,8},{24,16},{0,24},{9,1},{17,9},{25,17},{1,25},{10,2},{18... | collective-permute-start | bytes 393224 | tf_op jit(solution)/shard_map/ppermute | solution.py:21
  34.7 5.8 %collective-permute-start.7 = (bf16[1,2,256,128]{3,2,1,0:T(8,128)(2,1)S(1)}, bf16[1,2,256,128]{3,2,1,0:T(8,128)(2,1)S(1)}, u32[]{:S(2)}, u32[]{:S(2)}) collective-permute-start(bf16[1,2,256,128]{3,2,1,0:T(8,128)(2,1)S(1)} %get-tuple-element.14), channel_id=1, source_target_pairs={{0,8},{8,16},{16,24},{24,0},{1,9},{9,17},{17,25},{25,1},{2,10},{10... | collective-permute-start | bytes 393224 | tf_op jit(solution)/shard_map/ppermute | solution.py:19
  46.6 2.9 %copy-start.2 = (bf16[4,256,128]{2,1,0:T(8,128)(2,1)S(1)}, bf16[4,256,128]{2,1,0:T(8,128)(2,1)}, u32[]{:S(2)}) copy-start(bf16[4,256,128]{2,1,0:T(8,128)(2,1)} %copy-done.1) | copy-start | bytes 786436
  46.6 2.9 %copy-start.4 = (bf16[2,2,1,256,128]{4,3,1,0,2:T(8,128)(2,1)S(1)}, bf16[2,2,1,256,128]{4,3,1,0,2:T(8,128)(2,1)}, u32[]{:S(2)}) copy-start(bf16[2,2,1,256,128]{4,3,1,0,2:T(8,128)(2,1)} %get-tuple-element.11) | copy-start | bytes 786436
  46.6 2.9 %copy-start.5 = (bf16[2,2,1,256,128]{4,3,1,0,2:T(8,128)(2,1)S(1)}, bf16[2,2,1,256,128]{4,3,1,0,2:T(8,128)(2,1)}, u32[]{:S(2)}) copy-start(bf16[2,2,1,256,128]{4,3,1,0,2:T(8,128)(2,1)} %get-tuple-element.12) | copy-start | bytes 786436
  46.6 2.9 %copy-start.12 = (pred[2,2]{1,0:T(4,128)(4,1)S(1)}, pred[2,2]{1,0:T(4,128)(4,1)}, u32[]{:S(2)}) copy-start(pred[2,2]{1,0:T(4,128)(4,1)} %copy-done.11) | copy-start | bytes 16
where the time goes:
time: 56.2 us; the launch traced here: 56 us
  waiting for transfers between devices  16.2 us (29%)
  matrix products  12.1 us (22%)
  starting transfers between devices  10.8 us (19%)
  other arithmetic  9.29 us (17%)
  local copies, waits for them, and re-layouts  7.42 us (13%)
    ppermute x4, starting transfers between devices, with_halo(): lax.ppermute(head, axis, [((i + 1) % count, i) for i in range(count)])  10.3 us
    ppermute x4, waiting for transfers between devices, with_halo(): lax.ppermute(head, axis, [((i + 1) % count, i) for i in range(count)])  8.57 us
    ppermute x4, waiting for transfers between devices, with_halo(): lax.ppermute(tail, axis, [(i, (i + 1) % count) for i in range(count)])  7.67 us
    select_n x2, other arithmetic, hop_terms(): spatial = jnp.take(source, neighbour_rows, axis=1)  5.67 us
    dot_general x2, matrix products, later_sweep(): jnp.einsum('tsnc,tscd->tsnd', difference, inverse_blocks, preferred_eleme...  5.03 us
    gather x2, local copies, waits for them, and re-layouts, hop_terms(): spatial = jnp.take(source, neighbour_rows, axis=1)  3.89 us
    dot_general x1, matrix products, body(): jnp.einsum('tsnr,tsrc->tsnc', fine_residual, basis, preferred_element_typ...  3.46 us
    dot_general x1, matrix products, body(): jnp.einsum('tsnc,tsrc->tsnr', gathered, basis, preferred_element_type=jnp...  3.31 us
  transfers between devices with their start and end apart: 8, of which 7 were waited for; matrix products, arithmetic and copies ran while one was open for 4% of the time, Pallas kernels for 0%

commit v1 on v0

v1 whole, which is shorter than its diff:
```python
import functools

import jax
import jax.numpy as jnp
from jax import lax
from jax.experimental import pallas as pl
from jax.experimental.pallas import tpu as pltpu
from jax.sharding import PartitionSpec as P

SWEEPS = 3
DAMPING = 0.8
CHUNKS = 4
LAG = 4
F32 = jnp.float32
BF16 = jnp.bfloat16


def dot(a, b):
    return jnp.dot(a, b, preferred_element_type=F32)


def sweep_kernel(
    chunks, lats, srcs, fine, basis, diag, hops, table, agg, out,
    fine_v, basis_v, diag_v, hops_v, rhs, acc, cells, from_partner, from_far, above, below, last,
    fine_sem, basis_sem, diag_sem, hops_sem, out_sem,
    partner_send, partner_recv, far_send, far_recv, above_send, above_recv, below_send, below_recv,
):
    times, sites, sources, _ = fine.shape
    rows = sources // chunks
    lat, src = lax.axis_index("lat"), lax.axis_index("src")
    later, earlier = lax.rem(lat + 1, lats), lax.rem(lat + lats - 1, lats)
    odd = lax.rem(src, 2)
    partner = src + 1 - 2 * odd
    far_target = lax.rem(src + 2 - 4 * odd + srcs, srcs)
    far_source = lax.rem(src - 2 + 4 * odd + srcs, srcs)

    barrier = pltpu.get_barrier_semaphore()
    for device in ((later, src), (earlier, src), (lat, partner), (lat, far_source)):
        pl.semaphore_signal(barrier, inc=1, device_id=device, device_id_type=pl.DeviceIdType.MESH)

    def span(c):
        return pl.ds(c * rows, rows)

    def load_fine(c, t, s):
        return pltpu.make_async_copy(
            fine.at[t, s, span(c)], fine_v.at[t, s, span(c)], fine_sem.at[c, t, s])

    def load_basis(t, s):
        return pltpu.make_async_copy(basis.at[t, s], basis_v.at[t, s], basis_sem.at[t, s])

    load_diag = pltpu.make_async_copy(diag, diag_v, diag_sem)
    load_hops = pltpu.make_async_copy(hops, hops_v, hops_sem)

    pieces = [(c, t) for c in range(chunks) for t in range(times)]
    for c, t in pieces:
        for s in range(sites):
            if c == 0:
                load_basis(t, s).start()
            load_fine(c, t, s).start()
        if c == 0 and t == 0:
            load_diag.start()
    load_hops.start()

    def remote(source, target, send, recv, device):
        return pltpu.make_async_remote_copy(
            src_ref=source, dst_ref=target, send_sem=send, recv_sem=recv,
            device_id=device, device_id_type=pl.DeviceIdType.MESH)

    def to_partner(x, c, t):
        return remote(cells.at[x, c, t], from_partner.at[x, c, t],
                      partner_send.at[x, c, t], partner_recv.at[x, c, t], (lat, partner))

    def to_far(x, c, t):
        return remote(from_partner.at[x, c, t], from_far.at[x, c, t],
                      far_send.at[x, c, t], far_recv.at[x, c, t], (lat, far_target))

    def to_later(x, c):
        return remote(cells.at[x, c, times - 1], below.at[x, c],
                      below_send.at[x, c], below_recv.at[x, c], (later, src))

    def to_earlier(x, c):
        return remote(cells.at[x, c, 0], above.at[x, c],
                      above_send.at[x, c], above_recv.at[x, c], (earlier, src))

    def send(x, c, t):
        to_partner(x, c, t).start()
        if t == times - 1:
            to_later(x, c).start()
        if t == 0:
            to_earlier(x, c).start()

    for c, t in pieces:
        coarse = []
        for s in range(sites):
            if c == 0:
                load_basis(t, s).wait()
            load_fine(c, t, s).wait()
            coarse.append(dot(fine_v[t, s, span(c)], basis_v[t, s]))
        if c == 0 and t == 0:
            load_diag.wait()
        swap = lax.rem(agg[t, 0], sites) == 1
        for s in range(sites):
            here = jnp.where(swap, coarse[1 - s], coarse[s]).astype(BF16)
            rhs[c, t, s] = here
            cells[0, c, t, s] = (DAMPING * dot(here, diag_v[t, s])).astype(BF16)
        if c == 0 and t == 0:
            pl.semaphore_wait(barrier, 4)
        send(0, c, t)
    load_hops.wait()

    def local_terms(x, c, t):
        for s in range(sites):
            own, other = cells[x, c, t, s], cells[x, c, t, 1 - s]
            total = dot(jnp.concatenate([own, own], axis=1), hops_v[t, s, 2:4].reshape(-1, own.shape[1]))
            total += dot(jnp.concatenate([other, other], axis=1), hops_v[t, s, 4:6].reshape(-1, own.shape[1]))
            if t + 1 < times:
                total += dot(cells[x, c, t + 1, s], hops_v[t, s, 6])
            if t > 0:
                total += dot(cells[x, c, t - 1, s], hops_v[t, s, 7])
            acc[c, t, s] = rhs[c, t, s].astype(F32) - total

    def forward(x, c, t):
        to_partner(x, c, t).wait_recv()
        to_far(x, c, t).start()

    def finish(x, c, t):
        if t == times - 1:
            to_earlier(x, c).wait_recv()
        if t == 0:
            to_later(x, c).wait_recv()
        to_far(x, c, t).wait_recv()
        for s in range(sites):
            site = src * sites + s
            near = partner * sites + s
            column = jnp.where(table[0, site] == near, 0, 1)
            total = dot(from_partner[x, c, t, s], hops_v[t, s, column])
            total += dot(from_far[x, c, t, s], hops_v[t, s, 1 - column])
            if t == times - 1:
                total += dot(above[x, c, s], hops_v[t, s, 6])
            if t == 0:
                total += dot(below[x, c, s], hops_v[t, s, 7])
            difference = (acc[c, t, s] - total).astype(BF16)
            applied = dot(difference, diag_v[t, s])
            new = ((1.0 - DAMPING) * cells[x, c, t, s].astype(F32) + DAMPING * applied).astype(BF16)
            if x + 1 < SWEEPS - 1:
                cells[x + 1, c, t, s] = new
            else:
                last[c, t, s] = new
        if x + 1 < SWEEPS - 1:
            send(x + 1, c, t)
            if t == times - 1:
                for each in range(times):
                    local_terms(x + 1, c, each)
        else:
            store(c, t).start()

    def store(c, t):
        return pltpu.make_async_copy(last.at[c, t], out.at[t, :, span(c)], out_sem.at[c, t])

    exchanges = SWEEPS - 1
    count = len(pieces)
    for step in range(count + LAG * (2 * exchanges - 1)):
        for x in range(exchanges):
            at = step - 2 * LAG * x
            if 0 <= at < count:
                forward(x, *pieces[at])
                if x == 0:
                    local_terms(0, *pieces[at])
            at -= LAG
            if 0 <= at < count:
                finish(x, *pieces[at])

    for c, t in pieces:
        for x in range(exchanges):
            to_partner(x, c, t).wait_send()
            to_far(x, c, t).wait_send()
            if t == times - 1:
                to_later(x, c).wait_send()
            if t == 0:
                to_earlier(x, c).wait_send()
        store(c, t).wait()


def prolong_kernel(agg, cells, basis, out, cells_v, basis_v, out_v, cells_sem, basis_sem, out_sem):
    times, sites, sources, _ = cells.shape
    blocks = [(t, s) for t in range(times) for s in range(sites)]
    parts = 2
    rows = sources // parts

    def load_basis(t, s):
        return pltpu.make_async_copy(basis.at[t, s], basis_v.at[t, s], basis_sem.at[t, s])

    def store(t, s, p):
        span = pl.ds(p * rows, rows)
        return pltpu.make_async_copy(out_v.at[t, s, span], out.at[t, s, span], out_sem.at[t, s, p])

    load_cells = pltpu.make_async_copy(cells, cells_v, cells_sem)
    load_cells.start()
    for t, s in blocks:
        load_basis(t, s).start()
    load_cells.wait()
    for t, s in blocks:
        load_basis(t, s).wait()
        coarse = lax.rem(agg[t, s], sites)
        for p in range(parts):
            span = pl.ds(p * rows, rows)
            out_v[t, s, span] = lax.dot_general(
                cells_v[t, coarse, span], basis_v[t, s], (((1,), (1,)), ((), ())),
                preferred_element_type=F32).astype(BF16)
            store(t, s, p).start()
    for t, s in blocks:
        for p in range(parts):
            store(t, s, p).wait()


def body(lats, srcs, fine, basis, diag, hops, table, agg):
    times, sites, sources, depth = fine.shape
    width = basis.shape[3]
    chunks, exchanges = CHUNKS, SWEEPS - 1
    rows = sources // chunks
    any_spec = pl.BlockSpec(memory_space=pl.ANY)
    smem_spec = pl.BlockSpec(memory_space=pltpu.SMEM)
    dma = pltpu.SemaphoreType.DMA
    piece = (sites, rows, width)
    per_piece, per_chunk = dma((exchanges, chunks, times)), dma((exchanges, chunks))
    cells = pl.pallas_call(
        functools.partial(sweep_kernel, chunks, lats, srcs),
        out_shape=jax.ShapeDtypeStruct((times, sites, sources, width), BF16),
        in_specs=[any_spec] * 4 + [smem_spec] * 2,
        out_specs=any_spec,
        scratch_shapes=[
            pltpu.VMEM(fine.shape, BF16),
            pltpu.VMEM(basis.shape, BF16),
            pltpu.VMEM(diag.shape, BF16),
            pltpu.VMEM(hops.shape, BF16),
            pltpu.VMEM((chunks, times) + piece, BF16),
            pltpu.VMEM((chunks, times) + piece, F32),
            pltpu.VMEM((exchanges, chunks, times) + piece, BF16),
            pltpu.VMEM((exchanges, chunks, times) + piece, BF16),
            pltpu.VMEM((exchanges, chunks, times) + piece, BF16),
            pltpu.VMEM((exchanges, chunks) + piece, BF16),
            pltpu.VMEM((exchanges, chunks) + piece, BF16),
            pltpu.VMEM((chunks, times) + piece, BF16),
            dma((chunks, times, sites)),
            dma((times, sites)),
            dma(()),
            dma(()),
            dma((chunks, times)),
            per_piece, per_piece, per_piece, per_piece,
            per_chunk, per_chunk, per_chunk, per_chunk,
        ],
        compiler_params=pltpu.CompilerParams(collective_id=0, has_side_effects=True),
        name="sweeps",
    )(fine, basis, diag, hops, table.T, agg)
    return pl.pallas_call(
        prolong_kernel,
        out_shape=jax.ShapeDtypeStruct(fine.shape, BF16),
        in_specs=[smem_spec, any_spec, any_spec],
        out_specs=any_spec,
        scratch_shapes=[
            pltpu.VMEM(cells.shape, BF16),
            pltpu.VMEM(basis.shape, BF16),
            pltpu.VMEM(fine.shape, BF16),
            dma(()),
            dma((times, sites)),
            dma((times, sites, 2)),
        ],
        name="prolong",
    )(agg, cells, basis)


def solution(mesh):
    return jax.shard_map(
        functools.partial(body, mesh.shape["lat"], mesh.shape["src"]),
        mesh=mesh,
        in_specs=(
            P("lat", "src", None, None),
            P("lat", "src", None, None),
            P("lat", "src", None, None),
            P("lat", "src", None, None, None),
            P(),
            P("lat", "src"),
        ),
        out_specs=P("lat", "src", None, None),
        check_vma=False,
    )
```

time: 56.2 us -> 34.3 us (0.61)
  Pallas kernels: 0 us -> 34.1 us
  waiting for transfers between devices: 16.2 us -> 0 us
  matrix products: 12.1 us -> 0 us
  starting transfers between devices: 10.8 us -> 0 us
  other arithmetic: 9.29 us -> 0 us
  local copies, waits for them, and re-layouts: 7.42 us -> 0 us
    pallas_call x0 -> x2, Pallas kernels: none -> 34.1 us  [the longest x1 29.3 us: body(): pl.pallas_call(functools.partial(sweep_kernel, chunks, lats, srcs), out_s...]
    ppermute x8 -> x0, waiting for transfers between devices: 16.2 us -> none  [the longest x4 8.57 us: with_halo(): lax.ppermute(head, axis, [((i + 1) % count, i) for i in range(count)])]
    dot_general x5 -> x0, matrix products: 12.1 us -> none  [the longest x2 5.03 us: later_sweep(): jnp.einsum('tsnc,tscd->tsnd', difference, inverse_blocks, preferred_eleme...]
    ppermute x8 -> x0, starting transfers between devices: 10.8 us -> none  [the longest x4 10.3 us: with_halo(): lax.ppermute(head, axis, [((i + 1) % count, i) for i in range(count)])]
    select_n x2 -> x0, other arithmetic: 5.67 us -> none  [hop_terms(): spatial = jnp.take(source, neighbour_rows, axis=1)]
    gather x6 -> x0, local copies, waits for them, and re-layouts: 5.25 us -> none  [the longest x2 3.89 us: hop_terms(): spatial = jnp.take(source, neighbour_rows, axis=1)]
    broadcast_in_dim x2 -> x0, other arithmetic: 1.69 us -> none  [hop_terms(): upper_time = padded[2:][:, :, None]]
    unnamed x27 -> x0, local copies, waits for them, and re-layouts: 1.66 us -> none
  transfers between devices with their start and end apart: 8 -> 0, of which waited for: 7 -> 0; matrix products, arithmetic and copies ran while one was open for 4% -> 0% of each run, Pallas kernels for 0% -> 0%
where the time goes in v1:
time: 34.3 us; the launch traced here: 34.1 us
  Pallas kernels  34.1 us (99%)
    pallas_call x1, Pallas kernels, body(): pl.pallas_call(functools.partial(sweep_kernel, chunks, lats, srcs), out_s...  29.3 us
    pallas_call x1, Pallas kernels, body(): pl.pallas_call(prolong_kernel, out_shape=jax.ShapeDtypeStruct(fine.shape,...  4.8 us

profile of v1, /device:TPU:0, one launch (start us, length us, event | category | flops | bytes accessed | tf_op | source)
XLA Modules:
  0.0 34.1 jit_solution(15179917020369976718)
XLA Ops:
  0.0 29.3 %sweeps.1.cells = bf16[2,2,256,128]{3,2,1,0:T(8,128)(2,1)} custom-call(bf16[2,2,256,2048]{3,2,1,0:T(8,128)(2,1)} %fine.1, bf16[2,2,2048,128]{3,2,1,0:T(8,128)(2,1)} %basis.3, bf16[2,2,128,128]{3,2,1,0:T(8,128)(2,1)} %diag.1, bf16[2,2,8,128,128]{4,3,2,1,0:T(8,128)(2,1)} %hops.1, s32[6,16]{1,0:T(8,128)} %bitcast.1, s32[2,2]{1,0:T(2,128)} %agg.3), custom_call_target="tpu_custom_call" | custom-call | tf_op jit(solution)/shard_map/sweeps/pallas_call | solution.py:226
  29.3 4.8 %prolong.1 = bf16[2,2,256,2048]{3,2,1,0:T(8,128)(2,1)} custom-call(s32[2,2]{1,0:T(2,128)} %agg.3, bf16[2,2,256,128]{3,2,1,0:T(8,128)(2,1)} %sweeps.1.cells, bf16[2,2,2048,128]{3,2,1,0:T(8,128)(2,1)} %basis.3), custom_call_target="tpu_custom_call" | custom-call | tf_op jit(solution)/shard_map/prolong/pallas_call | solution.py:255

commit v2 on v1

--- a/solution.py
+++ b/solution.py
@@ -11,6 +11,7 @@
 DAMPING = 0.8
 CHUNKS = 4
 LAG = 4
+STORES = 2
 F32 = jnp.float32
 BF16 = jnp.bfloat16
 
@@ -20,9 +21,9 @@
 
 
 def sweep_kernel(
-    chunks, lats, srcs, fine, basis, diag, hops, table, agg, out,
-    fine_v, basis_v, diag_v, hops_v, rhs, acc, cells, from_partner, from_far, above, below, last,
-    fine_sem, basis_sem, diag_sem, hops_sem, out_sem,
+    chunks, lats, srcs, fine, basis, diag, hops, table, agg, last, basis_v,
+    fine_v, diag_v, hops_v, rhs, acc, cells, from_partner, from_far, above, below,
+    fine_sem, basis_sem, diag_sem, hops_sem,
     partner_send, partner_recv, far_send, far_recv, above_send, above_recv, below_send, below_recv,
 ):
     times, sites, sources, _ = fine.shape
@@ -51,7 +52,7 @@
     load_diag = pltpu.make_async_copy(diag, diag_v, diag_sem)
     load_hops = pltpu.make_async_copy(hops, hops_v, hops_sem)
 
-    pieces = [(c, t) for c in range(chunks) for t in range(times)]
+    pieces = [(c, t) for t in range(times) for c in range(chunks)]
     for c, t in pieces:
         for s in range(sites):
             if c == 0:
@@ -90,19 +91,19 @@
             to_earlier(x, c).start()
 
     for c, t in pieces:
-        coarse = []
         for s in range(sites):
             if c == 0:
                 load_basis(t, s).wait()
             load_fine(c, t, s).wait()
-            coarse.append(dot(fine_v[t, s, span(c)], basis_v[t, s]))
         if c == 0 and t == 0:
             load_diag.wait()
+        coarse = [dot(fine_v[t, s, span(c)], basis_v[t, s]) for s in range(sites)]
         swap = lax.rem(agg[t, 0], sites) == 1
-        for s in range(sites):
-            here = jnp.where(swap, coarse[1 - s], coarse[s]).astype(BF16)
-            rhs[c, t, s] = here
-            cells[0, c, t, s] = (DAMPING * dot(here, diag_v[t, s])).astype(BF16)
+        here = [jnp.where(swap, coarse[1 - s], coarse[s]).astype(BF16) for s in range(sites)]
+        applied = [dot(here[s], diag_v[t, s]) for s in range(sites)]
+        for s in range(sites):
+            cells[0, c, t, s] = (DAMPING * applied[s]).astype(BF16)
+            rhs[c, t, s] = here[s]
         if c == 0 and t == 0:
             pl.semaphore_wait(barrier, 4)
         send(0, c, t)
@@ -129,33 +130,29 @@
         if t == 0:
             to_later(x, c).wait_recv()
         to_far(x, c, t).wait_recv()
-        for s in range(sites):
-            site = src * sites + s
-            near = partner * sites + s
-            column = jnp.where(table[0, site] == near, 0, 1)
+        totals = []
+        for s in range(sites):
+            column = jnp.where(table[0, src * sites + s] == partner * sites + s, 0, 1)
             total = dot(from_partner[x, c, t, s], hops_v[t, s, column])
             total += dot(from_far[x, c, t, s], hops_v[t, s, 1 - column])
             if t == times - 1:
                 total += dot(above[x, c, s], hops_v[t, s, 6])
             if t == 0:
                 total += dot(below[x, c, s], hops_v[t, s, 7])
-            difference = (acc[c, t, s] - total).astype(BF16)
-            applied = dot(difference, diag_v[t, s])
-            new = ((1.0 - DAMPING) * cells[x, c, t, s].astype(F32) + DAMPING * applied).astype(BF16)
+            totals.append(total)
+        differences = [(acc[c, t, s] - totals[s]).astype(BF16) for s in range(sites)]
+        applied = [dot(differences[s], diag_v[t, s]) for s in range(sites)]
+        for s in range(sites):
+            new = ((1.0 - DAMPING) * cells[x, c, t, s].astype(F32) + DAMPING * applied[s]).astype(BF16)
             if x + 1 < SWEEPS - 1:
                 cells[x + 1, c, t, s] = new
             else:
-                last[c, t, s] = new
+                last[t, s, span(c)] = new
         if x + 1 < SWEEPS - 1:
             send(x + 1, c, t)
             if t == times - 1:
                 for each in range(times):
                     local_terms(x + 1, c, each)
-        else:
-            store(c, t).start()
-
-    def store(c, t):
-        return pltpu.make_async_copy(last.at[c, t], out.at[t, :, span(c)], out_sem.at[c, t])
 
     exchanges = SWEEPS - 1
     count = len(pieces)
@@ -178,39 +175,25 @@
                 to_later(x, c).wait_send()
             if t == 0:
                 to_earlier(x, c).wait_send()
-        store(c, t).wait()
-
-
-def prolong_kernel(agg, cells, basis, out, cells_v, basis_v, out_v, cells_sem, basis_sem, out_sem):
+
+
+def prolong_kernel(agg, cells, basis, out, out_v, out_sem):
     times, sites, sources, _ = cells.shape
-    blocks = [(t, s) for t in range(times) for s in range(sites)]
-    parts = 2
-    rows = sources // parts
-
-    def load_basis(t, s):
-        return pltpu.make_async_copy(basis.at[t, s], basis_v.at[t, s], basis_sem.at[t, s])
+    blocks = [(t, s, p) for t in range(times) for s in range(sites) for p in range(STORES)]
+    rows = sources // STORES
 
     def store(t, s, p):
         span = pl.ds(p * rows, rows)
         return pltpu.make_async_copy(out_v.at[t, s, span], out.at[t, s, span], out_sem.at[t, s, p])
 
-    load_cells = pltpu.make_async_copy(cells, cells_v, cells_sem)
-    load_cells.start()
-    for t, s in blocks:
-        load_basis(t, s).start()
-    load_cells.wait()
-    for t, s in blocks:
-        load_basis(t, s).wait()
-        coarse = lax.rem(agg[t, s], sites)
-        for p in range(parts):
-            span = pl.ds(p * rows, rows)
-            out_v[t, s, span] = lax.dot_general(
-                cells_v[t, coarse, span], basis_v[t, s], (((1,), (1,)), ((), ())),
-                preferred_element_type=F32).astype(BF16)
-            store(t, s, p).start()
-    for t, s in blocks:
-        for p in range(parts):
-            store(t, s, p).wait()
+    for t, s, p in blocks:
+        span = pl.ds(p * rows, rows)
+        out_v[t, s, span] = lax.dot_general(
+            cells[t, lax.rem(agg[t, s], sites), span], basis[t, s], (((1,), (1,)), ((), ())),
+            preferred_element_type=F32).astype(BF16)
+        store(t, s, p).start()
+    for t, s, p in blocks:
+        store(t, s, p).wait()
 
 
 def body(lats, srcs, fine, basis, diag, hops, table, agg):
@@ -219,18 +202,18 @@
     chunks, exchanges = CHUNKS, SWEEPS - 1
     rows = sources // chunks
     any_spec = pl.BlockSpec(memory_space=pl.ANY)
+    vmem_spec = pl.BlockSpec(memory_space=pltpu.VMEM)
     smem_spec = pl.BlockSpec(memory_space=pltpu.SMEM)
     dma = pltpu.SemaphoreType.DMA
     piece = (sites, rows, width)
     per_piece, per_chunk = dma((exchanges, chunks, times)), dma((exchanges, chunks))
-    cells = pl.pallas_call(
+    cells, basis = pl.pallas_call(
         functools.partial(sweep_kernel, chunks, lats, srcs),
-        out_shape=jax.ShapeDtypeStruct((times, sites, sources, width), BF16),
+        out_shape=[pltpu.VMEM((times, sites, sources, width), BF16), pltpu.VMEM(basis.shape, BF16)],
         in_specs=[any_spec] * 4 + [smem_spec] * 2,
-        out_specs=any_spec,
+        out_specs=[vmem_spec] * 2,
         scratch_shapes=[
             pltpu.VMEM(fine.shape, BF16),
-            pltpu.VMEM(basis.shape, BF16),
             pltpu.VMEM(diag.shape, BF16),
             pltpu.VMEM(hops.shape, BF16),
             pltpu.VMEM((chunks, times) + piece, BF16),
@@ -240,31 +223,24 @@
             pltpu.VMEM((exchanges, chunks, times) + piece, BF16),
             pltpu.VMEM((exchanges, chunks) + piece, BF16),
             pltpu.VMEM((exchanges, chunks) + piece, BF16),
-            pltpu.VMEM((chunks, times) + piece, BF16),
             dma((chunks, times, sites)),
             dma((times, sites)),
             dma(()),
             dma(()),
-            dma((chunks, times)),
             per_piece, per_piece, per_piece, per_piece,
             per_chunk, per_chunk, per_chunk, per_chunk,
         ],
         compiler_params=pltpu.CompilerParams(collective_id=0, has_side_effects=True),
         name="sweeps",
     )(fine, basis, diag, hops, table.T, agg)
+    cells = pltpu.with_memory_space_constraint(cells, pltpu.VMEM)
+    basis = pltpu.with_memory_space_constraint(basis, pltpu.VMEM)
     return pl.pallas_call(
         prolong_kernel,
         out_shape=jax.ShapeDtypeStruct(fine.shape, BF16),
-        in_specs=[smem_spec, any_spec, any_spec],
+        in_specs=[smem_spec, vmem_spec, vmem_spec],
         out_specs=any_spec,
-        scratch_shapes=[
-            pltpu.VMEM(cells.shape, BF16),
-            pltpu.VMEM(basis.shape, BF16),
-            pltpu.VMEM(fine.shape, BF16),
-            dma(()),
-            dma((times, sites)),
-            dma((times, sites, 2)),
-        ],
+        scratch_shapes=[pltpu.VMEM(fine.shape, BF16), dma((times, sites, STORES))],
         name="prolong",
     )(agg, cells, basis)
 

time: 34.3 us -> 30.5 us (0.89)
  Pallas kernels: 34.1 us -> 30.3 us
    pallas_call x1, Pallas kernels: 29.3 us -> 27.3 us  [body(): pl.pallas_call(functools.partial(sweep_kernel, chunks, lats, srcs), out_s...]
    pallas_call x1, Pallas kernels: 4.8 us -> 3.06 us  [body(): pl.pallas_call(prolong_kernel, out_shape=jax.ShapeDtypeStruct(fine.shape,...]
where the time goes in v2:
time: 30.5 us; the launch traced here: 30.3 us
  Pallas kernels  30.3 us (99%)
    pallas_call x1, Pallas kernels, body(): pl.pallas_call(functools.partial(sweep_kernel, chunks, lats, srcs), out_s...  27.3 us
    pallas_call x1, Pallas kernels, body(): pl.pallas_call(prolong_kernel, out_shape=jax.ShapeDtypeStruct(fine.shape,...  3.06 us

profile of v2, /device:TPU:0, one launch (start us, length us, event | category | flops | bytes accessed | tf_op | source)
XLA Modules:
  0.0 30.3 jit_solution(1839019550149051679)
XLA Ops:
  0.0 27.3 %sweeps.1 = (bf16[2,2,256,128]{3,2,1,0:T(8,128)(2,1)S(1)}, bf16[2,2,2048,128]{3,2,1,0:T(8,128)(2,1)S(1)}) custom-call(bf16[2,2,256,2048]{3,2,1,0:T(8,128)(2,1)} %fine.1, bf16[2,2,2048,128]{3,2,1,0:T(8,128)(2,1)} %basis.1, bf16[2,2,128,128]{3,2,1,0:T(8,128)(2,1)} %diag.1, bf16[2,2,8,128,128]{4,3,2,1,0:T(8,128)(2,1)} %hops.1, s32[6,16]{1,0:T(8,128)} %bitcast.1, ...), custom_call_target="tpu_custom_call" | custom-call | tf_op jit(solution)/shard_map/sweeps/pallas_call | solution.py:210
  27.3 3.1 %prolong.1 = bf16[2,2,256,2048]{3,2,1,0:T(8,128)(2,1)} custom-call(s32[2,2]{1,0:T(2,128)} %agg.3, bf16[2,2,256,128]{3,2,1,0:T(8,128)(2,1)S(1)} %get-tuple-element.7.cells, bf16[2,2,2048,128]{3,2,1,0:T(8,128)(2,1)S(1)} %get-tuple-element.8.basis), custom_call_target="tpu_custom_call" | custom-call | tf_op jit(solution)/shard_map/prolong/pallas_call | solution.py:238

commit v3 on v2

--- a/solution.py
+++ b/solution.py
@@ -9,7 +9,7 @@
 
 SWEEPS = 3
 DAMPING = 0.8
-CHUNKS = 4
+CHUNKS = 2
 LAG = 4
 STORES = 2
 F32 = jnp.float32

time: 30.5 us -> 30.1 us (0.987)
  Pallas kernels: 30.3 us -> 29.8 us
    pallas_call x1, Pallas kernels: 27.3 us -> 26.8 us  [body(): pl.pallas_call(functools.partial(sweep_kernel, chunks, lats, srcs), out_s...]
where the time goes in v3:
time: 30.1 us; the launch traced here: 29.9 us
  Pallas kernels  29.8 us (99%)
    pallas_call x1, Pallas kernels, body(): pl.pallas_call(functools.partial(sweep_kernel, chunks, lats, srcs), out_s...  26.8 us
    pallas_call x1, Pallas kernels, body(): pl.pallas_call(prolong_kernel, out_shape=jax.ShapeDtypeStruct(fine.shape,...  3.06 us

profile of v3, /device:TPU:0, one launch (start us, length us, event | category | flops | bytes accessed | tf_op | source)
XLA Modules:
  0.0 29.9 jit_solution(4046740979413470455)
XLA Ops:
  0.0 26.8 %sweeps.1 = (bf16[2,2,256,128]{3,2,1,0:T(8,128)(2,1)S(1)}, bf16[2,2,2048,128]{3,2,1,0:T(8,128)(2,1)S(1)}) custom-call(bf16[2,2,256,2048]{3,2,1,0:T(8,128)(2,1)} %fine.1, bf16[2,2,2048,128]{3,2,1,0:T(8,128)(2,1)} %basis.1, bf16[2,2,128,128]{3,2,1,0:T(8,128)(2,1)} %diag.1, bf16[2,2,8,128,128]{4,3,2,1,0:T(8,128)(2,1)} %hops.1, s32[6,16]{1,0:T(8,128)} %bitcast.1, ...), custom_call_target="tpu_custom_call" | custom-call | tf_op jit(solution)/shard_map/sweeps/pallas_call | solution.py:210
  26.8 3.1 %prolong.1 = bf16[2,2,256,2048]{3,2,1,0:T(8,128)(2,1)} custom-call(s32[2,2]{1,0:T(2,128)} %agg.3, bf16[2,2,256,128]{3,2,1,0:T(8,128)(2,1)S(1)} %get-tuple-element.7.cells, bf16[2,2,2048,128]{3,2,1,0:T(8,128)(2,1)S(1)} %get-tuple-element.8.basis), custom_call_target="tpu_custom_call" | custom-call | tf_op jit(solution)/shard_map/prolong/pallas_call | solution.py:238
